TPU v7x, 256 devices: a whole 4x4x8 slice. The times are simulated.
256 devices in a mesh: expert: 32 (over z, x), col: 8 (over y, core).
Axes of the slice: x: 4, y: 4, z: 8, core: 2. Of those that a mesh axis runs over, the one named last changes fastest.
Arguments:
- tokens: bfloat16 [4096, 4096], P('expert', 'col'), may hold values from -6 to 6
- routes: int32 [4096, 8], P('expert'), may hold values from 0 to 63, all different within a row; in each aligned block of 128 rows (0 to 127, 128 to 255, ...) at most 24 rows name the same one
- route_weight: float32 [4096, 8], P('expert'), may hold values from 0.02 to 0.25
- language: int32 [4096], P('expert'), may hold values from 0 to 118
- lang_weight: float32 [119], replicated, may hold values from 0.01 to 0.1
- w_gate: bfloat16 [64, 1536, 4096], P('expert', 'col'), may hold values from -0.09375 to 0.09375
- w_up: bfloat16 [64, 1536, 4096], P('expert', 'col'), may hold values from -0.09375 to 0.09375
- w_down: bfloat16 [64, 1536, 4096], P('expert', None, 'col'), may hold values from -0.15625 to 0.15625
Outputs:
- layer_out: bfloat16 [4096, 4096], P('expert', 'col')
- gram: float32 [64, 1536, 1536], P('expert', 'col')
Inputs may be any that keep to these rules, and one draw needn't show every extreme that they name: `routes`: each row names 8 different experts. In each aligned block of 128 rows no expert is named by more than 24 rows, a bound that some block reaches.
All inputs are finite; a program needn't handle non-finite values.
Results may differ from a plain program's by a relative error of at most 0.0063.
Values may be sent and summed in bfloat16 or wider, within the bound.
A program may use at most 128 MiB of HBM per device.

v0:
```python
import jax
import jax.numpy as jnp
from jax import lax
from jax.sharding import PartitionSpec as P


def on_device(tokens, routes, route_weight, language, lang_weight, w_gate, w_up, w_down):
    tok_rows = routes.shape[0]
    top_count = routes.shape[1]
    local_exp = w_gate.shape[0]
    owners = lax.axis_size("expert")
    experts = local_exp * owners
    capacity = tok_rows * top_count * 3 // (2 * experts)
    expert_ids = jnp.arange(experts, dtype=jnp.int32)
    chosen = routes[:, :, None] == expert_ids[None, None, :]
    hits = jnp.any(chosen, axis=1).astype(jnp.int32)
    coefs = jnp.sum(jnp.where(chosen, route_weight[:, :, None], jnp.zeros((), jnp.float32)), axis=1)
    places = jnp.cumsum(hits, axis=0) - hits
    slot_ids = jnp.arange(capacity, dtype=jnp.int32)
    picks = (hits.T[:, None, :] == 1) & (places.T[:, None, :] == slot_ids[None, :, None])
    row_index = jnp.arange(tok_rows, dtype=jnp.int32)
    slot_token = jnp.sum(jnp.where(picks, row_index[None, None, :], 0), axis=2)
    filled = jnp.any(picks, axis=2)
    lang_table = language[:, None] == jnp.arange(lang_weight.shape[0], dtype=jnp.int32)[None, :]
    calib = jnp.sum(
        jnp.where(lang_table, lang_weight[None, :], jnp.zeros((), jnp.float32)), axis=1
    ).astype(jnp.bfloat16)
    slot_cal = jnp.where(filled, calib[slot_token], jnp.zeros((), jnp.bfloat16)).reshape(
        owners, local_exp, capacity
    )
    slot_coef = jnp.where(
        filled, jnp.take_along_axis(coefs.T, slot_token, axis=1), jnp.zeros((), jnp.float32)
    )
    flat_token = slot_token.reshape(-1)
    flat_filled = filled.reshape(-1)
    whole = lax.all_gather(tokens, "col", axis=1, tiled=True)
    rows = jnp.take(whole, flat_token, axis=0)
    rows = jnp.where(flat_filled[:, None], rows, jnp.zeros((), jnp.bfloat16))
    arrived = lax.all_to_all(
        rows.reshape(owners, local_exp, capacity, whole.shape[1]),
        "expert",
        split_axis=0,
        concat_axis=0,
        tiled=True,
    )
    arrived_cal = lax.all_to_all(slot_cal, "expert", split_axis=0, concat_axis=0, tiled=True)
    gate = jnp.einsum("seck,efk->escf", arrived, w_gate, preferred_element_type=jnp.float32)
    upper = jnp.einsum("seck,efk->escf", arrived, w_up, preferred_element_type=jnp.float32)
    hidden = (jax.nn.silu(gate) * upper).astype(jnp.bfloat16)
    cal_rows = jnp.transpose(arrived_cal, (1, 0, 2))
    scaled = (cal_rows[..., None].astype(jnp.float32) * hidden.astype(jnp.float32)).astype(
        jnp.bfloat16
    )
    d_local = w_down.shape[2]
    piece = lax.all_gather(hidden, "col", axis=3, tiled=True)
    block = jnp.einsum("escu,escv->euv", scaled, piece, preferred_element_type=jnp.float32)
    mixed_now = jnp.einsum("escv,evd->escd", piece, w_down, preferred_element_type=jnp.float32)
    expert_out = mixed_now.astype(jnp.bfloat16)
    returned = lax.all_to_all(expert_out, "expert", split_axis=1, concat_axis=0, tiled=True)
    returned = returned.reshape(experts * capacity, d_local).astype(jnp.float32)
    combined = jnp.zeros((tok_rows, d_local), jnp.float32)
    combined = combined.at[flat_token].add(slot_coef.reshape(-1)[:, None] * returned)
    return (combined.astype(jnp.bfloat16), block)


def solution(mesh):
    in_specs = (
        P("expert", "col"),
        P("expert", None),
        P("expert", None),
        P("expert"),
        P(),
        P("expert", "col", None),
        P("expert", "col", None),
        P("expert", None, "col"),
    )
    out_specs = (P("expert", "col"), P("expert", "col", None))
    return jax.shard_map(
        on_device, mesh=mesh, in_specs=in_specs, out_specs=out_specs, check_vma=False
    )
```

profile of v0, /device:TPU:1, one launch (start us, length us, event | category | flops | bytes accessed | tf_op | source)
XLA Modules:
  0.0 569.8 jit_solution(8276990550696766480)
XLA Ops:
  7.2 0.7 all-gather.3.cloned.1.call-update
  8.0 0.9 fusion.18
  9.3 1.2 select_reduce_fusion
  10.6 1.2 fusion.17
  11.9 28.2 %all-gather.3.cloned.1.call-done = bf16[128,4096]{1,0:T(8,128)(2,1)} async-done(((bf16[128,512]{1,0:T(8,128)(2,1)}), bf16[128,4096]{1,0:T(8,128)(2,1)}) %all-gather.3.cloned.1.call-update) | async-done | bytes 1048592 | tf_op jit(solution)/shard_map/all_gather | solution.py:36
  40.1 23.4 %gather_fusion = bf16[1536,4096]{1,0:T(8,128)(2,1)} fusion(bf16[128,4096]{1,0:T(8,128)(2,1)} %all-gather.3.cloned.1.call-done, s32[2048]{0:T(1024)S(1)} %pad_clamp_fusion.1), kind=kCustom, calls=%fused_computation | custom fusion | bytes 25171968 | tf_op jit(solution)/shard_map/jit(_take)/gather | solution.py:37
  63.5 6.7 %select_select_fusion = bf16[32,2,24,4096]{3,2,1,0:T(8,128)(2,1)S(1)} fusion(bf16[32,2,24,4096]{3,2,1,0:T(8,128)(2,1)} %bitcast.49, pred[32,2,24]{2,1,0:T(4,128)(4,1)S(1)} %compare_and_fusion, pred[32,2,24]{2,1,0:T(4,128)(4,1)S(1)} %broadcast_in_dim.95), kind=kLoop, calls=%fused_computation.4 | loop fusion | flops 12582912 | bytes 25168896 | tf_op jit(solution)/shard_map/jit(_where)/select_n | solution.py:38
  70.2 283.7 %all_to_all.19 = bf16[32,2,24,4096]{3,2,1,0:T(8,128)(2,1)} all-to-all(bf16[32,2,24,4096]{3,2,1,0:T(8,128)(2,1)S(1)} %select_select_fusion), channel_id=1, replica_groups=mesh['expert'=32,'col'=8] {'expert'}, dimensions={0} | all-to-all | bytes 25165824 | tf_op jit(solution)/shard_map/all_to_all | solution.py:39
  353.9 10.0 %fusion.2 = f32[2,32,24,192]{3,2,1,0:T(8,128)} fusion(bf16[32,2,24,4096]{3,2,1,0:T(8,128)(2,1)} %all_to_all.19, bf16[2,192,4096]{2,1,0:T(8,128)(2,1)} %param.13), kind=kOutput, calls=%fused_computation.7 | convolution fusion | flops 2415919104 | bytes 16908288 | tf_op jit(solution)/shard_map/seck,efk->escf/dot_general | solution.py:47
  363.9 10.5 %multiply_convert_fusion.1 = bf16[2,32,24,192]{3,2,1,0:T(8,128)(2,1)} fusion(f32[2,32,24,192]{3,2,1,0:T(8,128)} %fusion.2, bf16[2,192,4096]{2,1,0:T(8,128)(2,1)} %param.14, bf16[32,2,24,4096]{3,2,1,0:T(8,128)(2,1)} %all_to_all.19), kind=kOutput, calls=%fused_computation.18 | convolution fusion | flops 2417688576 | bytes 17498112 | tf_op jit(solution)/shard_map/seck,efk->escf/dot_general | solution.py:48
  374.4 3.7 copy.44
  378.4 9.0 %gather_fusion.1 = bf16[1536]{0:T(1024)(128)(2,1)S(1)} fusion(bf16[128]{0:T(256)(128)(2,1)S(1)} %select_reduce_fusion.2, s32[2048]{0:T(1024)S(1)} %pad_clamp_fusion), kind=kCustom, calls=%fused_computation.1 | custom fusion | bytes 12288 | tf_op jit(solution)/shard_map/gather | solution.py:28
  388.1 5.9 %all-to-all-start.2 = ((bf16[32,2,24]{2,1,0:T(2,128)(2,1)}), bf16[32,2,24]{2,1,0:T(2,128)(2,1)S(1)}, u32[]{:S(2)}, u32[]{:S(2)}) async-start(bf16[32,2,24]{2,1,0:T(2,128)(2,1)} %broadcast_select_fusion), calls=%async_computation.2 | async-start | bytes 32768 | tf_op jit(solution)/shard_map/all_to_all | solution.py:46
  394.0 77.9 %all-gather.5.cloned.1.call-done = bf16[2,32,24,1536]{1,2,0,3:T(8,128)(2,1)} async-done(((bf16[2,32,24,192]{1,2,0,3:T(8,128)(2,1)}), bf16[2,32,24,1536]{1,2,0,3:T(8,128)(2,1)}) %all-gather.5.cloned.1.call-update) | async-done | bytes 4718608 | tf_op jit(solution)/shard_map/all_gather | solution.py:55
  471.9 22.1 %copy.45 = bf16[2,32,24,1536]{3,2,1,0:T(8,128)(2,1)} copy(bf16[2,32,24,1536]{1,2,0,3:T(8,128)(2,1)} %all-gather.5.cloned.1.call-done) | data formatting | bytes 9437184 | tf_op jit(solution)/shard_map/all_gather | solution.py:55
  494.0 5.0 fusion.8
  499.1 1.3 copy.46
  500.4 9.6 %all-to-all-start.1 = ((bf16[2,32,24,512]{3,2,0,1:T(8,128)(2,1)}), bf16[2,32,24,512]{3,2,0,1:T(8,128)(2,1)}, u32[]{:S(2)}, u32[]{:S(2)}) async-start(bf16[2,32,24,512]{3,2,0,1:T(8,128)(2,1)} %copy.46), calls=%async_computation.1 | async-start | bytes 3145728 | tf_op jit(solution)/shard_map/all_to_all | solution.py:59
  510.5 10.7 %gather_fusion.2 = f32[1536]{0:T(1024)S(1)} fusion(f32[64,128]{0,1:T(8,128)S(1)} %bitcast.48, s32[1536]{0:T(1024)S(1)} %reshape.137), kind=kCustom, calls=%fused_computation.2 | custom fusion | bytes 24576 | tf_op jit(solution)/shard_map/jit(take_along_axis)/gather | solution.py:32
  521.2 5.2 convolution_bitcast_fusion
  526.4 21.6 %all-to-all-done.1 = bf16[2,32,24,512]{3,2,0,1:T(8,128)(2,1)} async-done(((bf16[2,32,24,512]{3,2,0,1:T(8,128)(2,1)}), bf16[2,32,24,512]{3,2,0,1:T(8,128)(2,1)}, u32[]{:S(2)}, u32[]{:S(2)}) %all-to-all-start.1) | async-done | bytes 1572896 | tf_op jit(solution)/shard_map/all_to_all | solution.py:59
  548.1 1.8 bitcast_convert_fusion
  549.9 1.9 bitcast_multiply_fusion
  551.8 10.4 %scatter_custom_fusion = f32[128,512]{1,0:T(8,128)S(1)} fusion(s32[1536]{0:T(1024)S(1)} %fusion.21, f32[1536,512]{1,0:T(8,128)} %bitcast_multiply_fusion, f32[]{:T(128)} %constant.16.clone.1), kind=kCustom, calls=%fused_computation.27 | custom fusion | flops 786432 | bytes 262656 | tf_op jit(solution)/shard_map/scatter-add | solution.py:62
  (40 shorter events, 2.8 us)
Async XLA Ops:
  7.2 486.8 %copy-start = (bf16[2,1536,512]{2,1,0:T(8,128)(2,1)S(1)}, bf16[2,1536,512]{2,1,0:T(8,128)(2,1)}, u32[]{:S(2)}) copy-start(bf16[2,1536,512]{2,1,0:T(8,128)(2,1)} %param.15) | copy-start | bytes 9437188
  7.2 32.9 %all-gather.3.cloned.1.call-start = ((), (), s32[]{:S(2)}) async-start(), calls=%async_computation.3 | async-start | bytes 1179648 | tf_op jit(solution)/shard_map/all_gather | solution.py:36
  7.9 464.0 %all-gather.5.cloned.1.call-start = ((), (), s32[]{:S(2)}) async-start(), calls=%async_computation.4 | async-start | bytes 21233664 | tf_op jit(solution)/shard_map/all_gather | solution.py:55
  374.4 3.8 copy-start.3
  374.4 3.8 copy-start.4
  388.1 112.3 %all-to-all-start.2 = ((bf16[32,2,24]{2,1,0:T(2,128)(2,1)}), bf16[32,2,24]{2,1,0:T(2,128)(2,1)S(1)}, u32[]{:S(2)}, u32[]{:S(2)}) async-start(bf16[32,2,24]{2,1,0:T(2,128)(2,1)} %broadcast_select_fusion), calls=%async_computation.2 | async-start | bytes 32768 | tf_op jit(solution)/shard_map/all_to_all | solution.py:46
  499.0 11.2 %copy-start.1 = (s32[128,8]{0,1:T(8,128)S(1)}, s32[128,8]{0,1:T(8,128)}, u32[]{:S(2)}) copy-start(s32[128,8]{0,1:T(8,128)} %param.9) | copy-start | bytes 12292
  499.0 11.2 %copy-start.2 = (f32[128,8]{0,1:T(8,128)S(1)}, f32[128,8]{0,1:T(8,128)}, u32[]{:S(2)}) copy-start(f32[128,8]{0,1:T(8,128)} %param.10) | copy-start | bytes 12292
  500.4 47.7 %all-to-all-start.1 = ((bf16[2,32,24,512]{3,2,0,1:T(8,128)(2,1)}), bf16[2,32,24,512]{3,2,0,1:T(8,128)(2,1)}, u32[]{:S(2)}, u32[]{:S(2)}) async-start(bf16[2,32,24,512]{3,2,0,1:T(8,128)(2,1)} %copy.46), calls=%async_computation.1 | async-start | bytes 3145728 | tf_op jit(solution)/shard_map/all_to_all | solution.py:59
Sparse Core Ops, SparseCore 0:
  9.8 30.1 all-gather.2
  378.2 93.6 all-gather.4
where the time goes:
time: 572 us; the launch traced here: 570 us
  blocking collectives  284 us (50%)
  waiting for transfers between devices  128 us (22%)
  local copies, waits for them, and re-layouts  71.1 us (12%)
  matrix products  30.7 us (5%)
  other arithmetic  25.9 us (5%)
  starting transfers between devices  15.6 us (3%)
  between operations  14.3 us (2%)
    all_to_all x1, blocking collectives, on_device(): lax.all_to_all(rows.reshape(owners, local_exp, capacity, whole.shape[1]),...  284 us
    all_gather x1, waiting for transfers between devices, on_device(): piece = lax.all_gather(hidden, 'col', axis=3, tiled=True)  77.9 us
    all_gather x1, waiting for transfers between devices, on_device(): whole = lax.all_gather(tokens, 'col', axis=1, tiled=True)  28.2 us
    gather x1, local copies, waits for them, and re-layouts, on_device(): rows = jnp.take(whole, flat_token, axis=0)  23.4 us
    all_gather x1, local copies, waits for them, and re-layouts, on_device(): piece = lax.all_gather(hidden, 'col', axis=3, tiled=True)  22.1 us
    all_to_all x1, waiting for transfers between devices, on_device(): lax.all_to_all(expert_out, 'expert', split_axis=1, concat_axis=0, tiled=T...  21.6 us
  transfers between devices with their start and end apart: 4, of which 3 were waited for; matrix products, arithmetic and copies ran while one was open for 10% of the time, Pallas kernels for 0%

commit v1 on v0

v1 whole, which is shorter than its diff:
```python
import jax
import jax.numpy as jnp
from jax import lax
from jax.experimental import pallas as pl
from jax.experimental.pallas import tpu as pltpu
from jax.sharding import PartitionSpec as P

MESH = pl.DeviceIdType.MESH
NZ, NX, NY = 8, 4, 4
TOK = 128
CAP = 24
PAIR = 2 * CAP
ROWS = NX * PAIR
CHUNKS = NZ // 2
D = 4096
DS = 512
FF = 1536
FS = 192
FC = 2 * FS
NSEM = 128

F32 = jnp.float32
BF16 = jnp.bfloat16


def kernel(
    tok_hbm, meta_hbm, wg_hbm, wu_hbm, wd_hbm,
    out_ref, gram_ref,
    tok, meta, pick_send, row_buf, cal_send, cal_buf, xs, w_in, w_dn,
    hid_own, scaled, hid, eo, back, coef_hi, coef_lo, part, part_in, gram,
    send_sem, recv_sem, local_sem,
):
    i = lax.axis_index("expert")
    c = lax.axis_index("col")
    z, x = i // NX, lax.rem(i, NX)
    y, k = c // 2, lax.rem(c, 2)
    other = 1 - k

    def at_z(step):
        return (lax.rem(z + step + NZ, NZ) * NX + x, c)

    def at_x(step, flip=0):
        core = other if flip else k
        return (z * NX + lax.rem(x + step + NX, NX), y * 2 + core)

    def at_y(step, flip=0):
        core = other if flip else k
        return (i, lax.rem(y + step + NY, NY) * 2 + core)

    sibling = (i, y * 2 + other)

    count = [0, 0]
    sent = []

    def remote(src, dst, device):
        n = count[0]
        count[0] += 1
        copy = pltpu.make_async_remote_copy(
            src_ref=src, dst_ref=dst, send_sem=send_sem.at[n], recv_sem=recv_sem.at[n],
            device_id=device, device_id_type=MESH,
        )
        copy.start()
        sent.append(copy)
        return copy

    def local(src, dst):
        n = count[1]
        count[1] += 1
        copy = pltpu.make_async_copy(src, dst, local_sem.at[n])
        copy.start()
        return copy

    def arrive(copies):
        for copy in copies:
            copy.wait_recv()

    own_tok = local(tok_hbm, tok.at[pl.ds(0, TOK), :])
    own_meta = local(meta_hbm, meta.at[0])
    own_rows = pl.ds(pl.multiple_of(k * FS, 64), FS)
    own_rows_up = pl.ds(pl.multiple_of(FC + k * FS, 64), FS)
    weights_local = [
        local(wg_hbm.at[k], w_in.at[own_rows, :]),
        local(wu_hbm.at[k], w_in.at[own_rows_up, :]),
        local(wd_hbm.at[k], w_dn.at[0]),
    ]

    barrier = pltpu.get_barrier_semaphore()
    partners = [at_z(s) for s in range(1, NZ)]
    partners += [at_x(s, f) for s in range(1, NX) for f in range(2)]
    partners += [at_y(s, f) for s in (-1, 1) for f in range(2)]
    partners += [sibling]
    for device in partners:
        pl.semaphore_signal(barrier, inc=1, device_id=device, device_id_type=MESH)
    pl.semaphore_wait(barrier, len(partners))

    def slot_of(offset):
        return 2 * offset if offset >= 0 else 2 * (-offset - 1) + 1

    def z_send(source, target, step):
        a, b = slot_of(source), slot_of(target)
        device = at_z(step)
        return [
            remote(tok.at[pl.ds(a * TOK, TOK), :], tok.at[pl.ds(b * TOK, TOK), :], device),
            remote(meta.at[a], meta.at[b], device),
        ]

    own_tok.wait()
    own_meta.wait()
    right = {1: z_send(0, -1, 1)}
    left = {1: z_send(0, 1, -1)}

    weights_remote = [
        remote(wg_hbm.at[other], w_in.at[own_rows, :], sibling),
        remote(wu_hbm.at[other], w_in.at[own_rows_up, :], sibling),
        remote(wd_hbm.at[other], w_dn.at[1], sibling),
    ]

    lane = lax.broadcasted_iota(jnp.int32, (2 * TOK, 2 * TOK), 1)
    sub = lax.broadcasted_iota(jnp.int32, (2 * TOK, 2 * TOK), 0)
    before = jnp.where((sub < lane) & (sub // TOK == lane // TOK), 1.0, 0.0).astype(BF16)
    block_base = jnp.where(
        lax.broadcasted_iota(jnp.int32, (1, 2 * TOK), 1) >= TOK, float(CAP), 0.0
    )
    row_id = lax.broadcasted_iota(jnp.int32, (PAIR, 2 * TOK), 0).astype(F32)

    picked, cal_in = {}, {}

    def stage_pick(p):
        arrive(right[p + 1])
        if p + 2 <= CHUNKS:
            right[p + 2] = z_send(-(p + 1), -(p + 2), 1)
        if p + 1 < CHUNKS:
            arrive(left[p + 1])
        if p + 2 < CHUNKS:
            left[p + 2] = z_send(p + 1, p + 2, -1)
        m0, m1 = meta[2 * p], meta[2 * p + 1]
        pair = jnp.concatenate([m0, m1], axis=1)
        experts, gains = pair[0:8], pair[8:16]
        cal = pair[16:17]
        hits, coefs = [], []
        for flip in range(2):
            for step in range(NX):
                e = (z * NX + lax.rem(x + step, NX)) * 2 + (other if flip else k)
                same = experts == e.astype(F32)
                hits.append(jnp.max(jnp.where(same, 1.0, 0.0), axis=0, keepdims=True))
                coefs.append(jnp.sum(jnp.where(same, gains, 0.0), axis=0, keepdims=True))
        hit = jnp.concatenate(hits, axis=0)
        place = jnp.dot(hit.astype(BF16), before, preferred_element_type=F32)
        where_to = jnp.where(hit > 0.5, place + block_base, -1.0)
        picks = []
        for g in range(2 * NX):
            mask = row_id == where_to[g : g + 1]
            picks.append(jnp.where(mask, 1.0, 0.0).astype(BF16))
            high = coefs[g].astype(BF16).astype(F32)
            coef_hi[p, pl.ds(g * PAIR, PAIR), :] = jnp.where(mask, high, 0.0).astype(BF16)
            coef_lo[p, pl.ds(g * PAIR, PAIR), :] = jnp.where(mask, coefs[g] - high, 0.0).astype(BF16)
            if g < NX:
                col = jnp.sum(jnp.where(mask, cal, 0.0), axis=1, keepdims=True)
                wide = jnp.broadcast_to(col, (PAIR, TOK)).astype(BF16)
                if g == 0:
                    cal_buf[pl.ds(p * ROWS, PAIR), :] = wide
                else:
                    cal_send[pl.ds(p * ROWS + g * PAIR, PAIR), :] = wide
        rows = jnp.dot(
            jnp.concatenate(picks, axis=0), tok[pl.ds(2 * p * TOK, 2 * TOK), :],
            preferred_element_type=F32,
        ).astype(BF16)
        for flip in range(2):
            mine = rows[flip * ROWS : (flip + 1) * ROWS]
            row_buf[flip, pl.ds(p * ROWS, PAIR), :] = mine[0:PAIR]
            pick_send[flip, pl.ds(p * ROWS, ROWS), :] = mine
        picked[p], cal_in[p] = [], []
        for step in range(1, NX):
            device = at_x(step)
            src = pl.ds(p * ROWS + step * PAIR, PAIR)
            dst = pl.ds(p * ROWS + (NX - step) * PAIR, PAIR)
            picked[p].append(remote(pick_send.at[:, src, :], row_buf.at[:, dst, :], device))
            cal_in[p].append(remote(cal_send.at[src, :], cal_buf.at[dst, :], device))

    own_lanes = pl.ds(pl.multiple_of(c * DS, DS), DS)
    own_hid = pl.ds(pl.multiple_of(y * FC, 128), FC)
    left_y, right_y = lax.rem(y + NY - 1, NY), lax.rem(y + 1, NY)
    direct, to_self, forwarded, kept = {}, {}, {}, {}

    def stage_spread(p):
        arrive(picked[p])
        rows = pl.ds(p * ROWS, ROWS)
        direct[p] = [
            remote(row_buf.at[flip, rows, :], xs.at[rows, own_lanes], at_y(step, flip))
            for flip in range(2) for step in (1, -1)
        ]
        to_self[p] = remote(row_buf.at[1, rows, :], xs.at[rows, own_lanes], sibling)
        kept[p] = local(row_buf.at[0, rows, :], xs.at[rows, own_lanes])

    def stage_forward(p):
        arrive(direct[p])
        half = ROWS // 2
        a = (pl.ds(p * ROWS, half), pl.ds(pl.multiple_of(left_y * 2 * DS, DS), 2 * DS))
        b = (pl.ds(p * ROWS + half, half), pl.ds(pl.multiple_of(right_y * 2 * DS, DS), 2 * DS))
        forwarded[p] = [
            remote(xs.at[a], xs.at[a], at_y(1)),
            remote(xs.at[b], xs.at[b], at_y(-1)),
        ]

    hid_direct, hid_forwarded, hid_kept = {}, {}, {}

    def stage_hidden(p):
        if p == 0:
            for copy in weights_local[:2]:
                copy.wait()
            arrive(weights_remote[:2])
        arrive(forwarded[p])
        to_self[p].wait_recv()
        kept[p].wait()
        arrive(cal_in[p])
        rows = pl.ds(p * ROWS, ROWS)
        both = lax.dot_general(
            xs[rows, :], w_in[...], (((1,), (1,)), ((), ())), preferred_element_type=F32
        )
        gate, up = both[:, 0:FC], both[:, FC : 2 * FC]
        h = (gate / (1.0 + jnp.exp(-gate)) * up).astype(BF16)
        hid_own[rows, :] = h
        hid_direct[p] = [
            remote(hid_own.at[rows, :], hid.at[rows, own_hid], at_y(step)) for step in (1, -1)
        ]
        hid_kept[p] = local(hid_own.at[rows, :], hid.at[rows, own_hid])
        cal = cal_buf[rows, :][:, 0:1].astype(F32)
        scaled[rows, :] = (cal * h.astype(F32)).astype(BF16)

    def stage_hidden_forward(p):
        arrive(hid_direct[p])
        half = ROWS // 2
        a = (pl.ds(p * ROWS, half), pl.ds(pl.multiple_of(left_y * FC, 128), FC))
        b = (pl.ds(p * ROWS + half, half), pl.ds(pl.multiple_of(right_y * FC, 128), FC))
        hid_forwarded[p] = [
            remote(hid.at[a], hid.at[a], at_y(1)),
            remote(hid.at[b], hid.at[b], at_y(-1)),
        ]

    returned, back_kept = {}, {}

    def stage_down(p):
        if p == 0:
            weights_local[2].wait()
            arrive(weights_remote[2:])
        arrive(hid_forwarded[p])
        hid_kept[p].wait()
        rows = pl.ds(p * ROWS, ROWS)
        for flip in range(2):
            eo[flip, rows, :] = jnp.dot(
                hid[rows, :], w_dn[flip], preferred_element_type=F32
            ).astype(BF16)
        returned[p] = []
        for step in range(NX):
            src = pl.ds(p * ROWS + step * PAIR, PAIR)
            dst = pl.ds(p * ROWS + (NX - step) % NX * PAIR, PAIR)
            for flip in range(2):
                if step == 0 and flip == 0:
                    back_kept[p] = local(eo.at[0, src, :], back.at[0, dst, :])
                else:
                    returned[p].append(
                        remote(eo.at[flip, src, :], back.at[flip, dst, :], at_x(step, flip))
                    )

    parts = []

    def stage_combine(p):
        arrive(returned[p])
        back_kept[p].wait()
        rows = back[:, pl.ds(p * ROWS, ROWS), :].reshape(2 * ROWS, DS)
        dims = (((0,), (0,)), ((), ()))
        total = lax.dot_general(coef_hi[p], rows, dims, preferred_element_type=F32)
        total = total + lax.dot_general(coef_lo[p], rows, dims, preferred_element_type=F32)
        part[pl.ds(2 * p * TOK, 2 * TOK), :] = total.astype(BF16)
        for b in range(2):
            if p == 0 and b == 0:
                continue
            s = pl.ds((2 * p + b) * TOK, TOK)
            offset = p if b == 0 else -(p + 1)
            parts.append(remote(part.at[s, :], part_in.at[s, :], at_z(offset)))

    grams = []

    def stage_gram():
        gram[...] = lax.dot_general(
            scaled[...], hid[...], (((0,), (0,)), ((), ())), preferred_element_type=F32
        )
        mine = pl.ds(pl.multiple_of(k * FS, 64), FS)
        theirs = pl.ds(pl.multiple_of(other * FS, 64), FS)
        grams.append(remote(gram.at[theirs, :], gram_ref.at[k], sibling))
        grams.append(local(gram.at[mine, :], gram_ref.at[k]))

    stage_pick(0)
    stage_pick(1)
    stage_spread(0)
    stage_pick(2)
    stage_spread(1)
    stage_pick(3)
    stage_forward(0)
    stage_spread(2)
    stage_forward(1)
    stage_hidden(0)
    stage_spread(3)
    stage_forward(2)
    stage_hidden_forward(0)
    stage_hidden(1)
    stage_down(0)
    stage_forward(3)
    stage_hidden_forward(1)
    stage_hidden(2)
    stage_combine(0)
    stage_down(1)
    stage_hidden_forward(2)
    stage_hidden(3)
    stage_combine(1)
    stage_down(2)
    stage_hidden_forward(3)
    stage_combine(2)
    stage_down(3)
    stage_gram()
    stage_combine(3)

    total = part[pl.ds(0, TOK), :].astype(F32)
    for n, copy in enumerate(parts):
        copy.wait_recv()
        total = total + part_in[pl.ds((n + 1) * TOK, TOK), :].astype(F32)
    out_ref[...] = total.astype(BF16)
    grams[0].wait_recv()
    grams[1].wait()
    for copy in sent:
        copy.wait_send()


def on_device(tokens, routes, route_weight, language, lang_weight, w_gate, w_up, w_down):
    langs = jnp.arange(lang_weight.shape[0], dtype=jnp.int32)
    cal = jnp.sum(jnp.where(language[None, :] == langs[:, None], lang_weight[:, None], 0.0), axis=0)
    meta = jnp.concatenate(
        [routes.T.astype(F32), route_weight.T, cal[None, :], jnp.zeros((7, TOK), F32)], axis=0
    )
    rows = CHUNKS * ROWS
    anywhere = pl.BlockSpec(memory_space=pl.ANY)
    return pl.pallas_call(
        kernel,
        out_shape=(
            jax.ShapeDtypeStruct((TOK, DS), BF16),
            jax.ShapeDtypeStruct((2, FS, FF), F32),
        ),
        in_specs=[anywhere] * 5,
        out_specs=(pl.BlockSpec(memory_space=pltpu.VMEM), anywhere),
        scratch_shapes=[
            pltpu.VMEM((NZ * TOK, DS), BF16),
            pltpu.VMEM((NZ, 24, TOK), F32),
            pltpu.VMEM((2, rows, DS), BF16),
            pltpu.VMEM((2, rows, DS), BF16),
            pltpu.VMEM((rows, TOK), BF16),
            pltpu.VMEM((rows, TOK), BF16),
            pltpu.VMEM((rows, D), BF16),
            pltpu.VMEM((2 * FC, D), BF16),
            pltpu.VMEM((2, FF, DS), BF16),
            pltpu.VMEM((rows, FC), BF16),
            pltpu.VMEM((rows, FC), BF16),
            pltpu.VMEM((rows, FF), BF16),
            pltpu.VMEM((2, rows, DS), BF16),
            pltpu.VMEM((2, rows, DS), BF16),
            pltpu.VMEM((CHUNKS, 2 * ROWS, 2 * TOK), BF16),
            pltpu.VMEM((CHUNKS, 2 * ROWS, 2 * TOK), BF16),
            pltpu.VMEM((NZ * TOK, DS), BF16),
            pltpu.VMEM((NZ * TOK, DS), BF16),
            pltpu.VMEM((FC, FF), F32),
            pltpu.SemaphoreType.DMA((NSEM,)),
            pltpu.SemaphoreType.DMA((NSEM,)),
            pltpu.SemaphoreType.DMA((24,)),
        ],
        compiler_params=pltpu.CompilerParams(
            collective_id=0, has_side_effects=True, vmem_limit_bytes=60 * 1024 * 1024
        ),
        name="routed_experts",
    )(tokens, meta, w_gate, w_up, w_down)


def solution(mesh):
    in_specs = (
        P("expert", "col"),
        P("expert", None),
        P("expert", None),
        P("expert"),
        P(),
        P("expert", "col", None),
        P("expert", "col", None),
        P("expert", None, "col"),
    )
    out_specs = (P("expert", "col"), P("expert", "col", None))
    return jax.shard_map(
        on_device, mesh=mesh, in_specs=in_specs, out_specs=out_specs, check_vma=False
    )
```

time: 572 us -> 140 us (0.24)
  blocking collectives: 284 us -> 0 us
  Pallas kernels: 0 us -> 131 us
  waiting for transfers between devices: 128 us -> 0 us
  local copies, waits for them, and re-layouts: 71.1 us -> 4.87 us
  matrix products: 30.7 us -> 0 us
  other arithmetic: 25.9 us -> 2.81 us
  starting transfers between devices: 15.6 us -> 0 us
  between operations: 14.3 us -> 0.65 us
    all_to_all x1 -> x0, blocking collectives: 284 us -> none  [on_device(): lax.all_to_all(rows.reshape(owners, local_exp, capacity, whole.shape[1]),...]
    pallas_call x0 -> x1, Pallas kernels: none -> 131 us  [on_device(): pl.pallas_call(kernel, out_shape=(jax.ShapeDtypeStruct((TOK, DS), BF16),...]
    all_gather x2 -> x0, waiting for transfers between devices: 106 us -> none  [the longest x1 77.9 us: on_device(): piece = lax.all_gather(hidden, 'col', axis=3, tiled=True)]
    gather x5 -> x0, local copies, waits for them, and re-layouts: 43.3 us -> none  [the longest x1 23.4 us: on_device(): rows = jnp.take(whole, flat_token, axis=0)]
    dot_general x4 -> x0, matrix products: 30.7 us -> none  [the longest x1 10.5 us: on_device(): jnp.einsum('seck,efk->escf', arrived, w_up, preferred_element_type=jnp.fl...]
    all_gather x1 -> x0, local copies, waits for them, and re-layouts: 22.1 us -> none  [on_device(): piece = lax.all_gather(hidden, 'col', axis=3, tiled=True)]
    all_to_all x2 -> x0, waiting for transfers between devices: 21.6 us -> none  [the longest x1 21.6 us: on_device(): lax.all_to_all(expert_out, 'expert', split_axis=1, concat_axis=0, tiled=T...]
    all_to_all x2 -> x0, starting transfers between devices: 15.6 us -> none  [the longest x1 9.65 us: on_device(): lax.all_to_all(expert_out, 'expert', split_axis=1, concat_axis=0, tiled=T...]
  transfers between devices with their start and end apart: 4 -> 0, of which waited for: 3 -> 0; matrix products, arithmetic and copies ran while one was open for 10% -> 0% of each run, Pallas kernels for 0% -> 0%
where the time goes in v1:
time: 140 us; the launch traced here: 139 us
  Pallas kernels  131 us (94%)
  local copies, waits for them, and re-layouts  4.87 us (3%)
  other arithmetic  2.81 us (2%)
    pallas_call x1, Pallas kernels, on_device(): pl.pallas_call(kernel, out_shape=(jax.ShapeDtypeStruct((TOK, DS), BF16),...  131 us
    unnamed x2, local copies, waits for them, and re-layouts  4.79 us

profile of v1, /device:TPU:1, one launch (start us, length us, event | category | flops | bytes accessed | tf_op | source)
XLA Modules:
  0.0 139.3 jit_solution(16294165919895820927)
XLA Ops:
  0.6 0.8 select_reduce_fusion
  1.4 0.1 pad.3.clone
  1.5 0.7 convert_bitcast_fusion
  2.2 1.4 maximum_maximum_fusion.meta_hbm
  3.5 131.0 %routed_experts.1 = (bf16[128,512]{1,0:T(8,128)(2,1)}, f32[2,192,1536]{2,1,0:T(8,128)}) custom-call(bf16[128,512]{1,0:T(8,128)(2,1)} %tok_hbm.1, f32[24,128]{1,0:T(8,128)} %maximum_maximum_fusion.meta_hbm, bf16[2,192,4096]{2,1,0:T(8,128)(2,1)} %wg_hbm.1, bf16[2,192,4096]{2,1,0:T(8,128)(2,1)} %wu_hbm.1, bf16[2,1536,512]{2,1,0:T(8,128)(2,1)} %wd_hbm.1), custom_call_target="tpu_custom_call" | custom-call | tf_op jit(solution)/shard_map/routed_experts/pallas_call | solution.py:342
  134.5 1.6 %copy.12 = bf16[128,512]{1,0:T(8,128)(2,1)} copy(bf16[128,512]{1,0:T(8,128)(2,1)} %get-tuple-element.4) | data formatting | bytes 262144
  136.1 3.2 %copy.13 = f32[2,192,1536]{2,1,0:T(8,128)} copy(f32[2,192,1536]{2,1,0:T(8,128)} %get-tuple-element.5) | data formatting | bytes 4718592
  (1 shorter events, 0.0 us)

commit v2 on v1

--- a/solution.py
+++ b/solution.py
@@ -12,12 +12,14 @@
 PAIR = 2 * CAP
 ROWS = NX * PAIR
 CHUNKS = NZ // 2
+HALF = ROWS // 2
+ORDER = (0, 2, 3, 1)
 D = 4096
 DS = 512
 FF = 1536
 FS = 192
 FC = 2 * FS
-NSEM = 128
+NSEM = 208
 
 F32 = jnp.float32
 BF16 = jnp.bfloat16
@@ -125,14 +127,15 @@
 
     picked, cal_in = {}, {}
 
+    def z_forward(hop):
+        arrive(right[hop])
+        if hop < CHUNKS:
+            right[hop + 1] = z_send(-hop, -(hop + 1), 1)
+            arrive(left[hop])
+        if hop + 1 < CHUNKS:
+            left[hop + 1] = z_send(hop, hop + 1, -1)
+
     def stage_pick(p):
-        arrive(right[p + 1])
-        if p + 2 <= CHUNKS:
-            right[p + 2] = z_send(-(p + 1), -(p + 2), 1)
-        if p + 1 < CHUNKS:
-            arrive(left[p + 1])
-        if p + 2 < CHUNKS:
-            left[p + 2] = z_send(p + 1, p + 2, -1)
         m0, m1 = meta[2 * p], meta[2 * p + 1]
         pair = jnp.concatenate([m0, m1], axis=1)
         experts, gains = pair[0:8], pair[8:16]
@@ -169,89 +172,96 @@
             mine = rows[flip * ROWS : (flip + 1) * ROWS]
             row_buf[flip, pl.ds(p * ROWS, PAIR), :] = mine[0:PAIR]
             pick_send[flip, pl.ds(p * ROWS, ROWS), :] = mine
-        picked[p], cal_in[p] = [], []
-        for step in range(1, NX):
+        picked[p], cal_in[p] = {}, {}
+        for step in (3, 1, 2):
             device = at_x(step)
             src = pl.ds(p * ROWS + step * PAIR, PAIR)
             dst = pl.ds(p * ROWS + (NX - step) * PAIR, PAIR)
-            picked[p].append(remote(pick_send.at[:, src, :], row_buf.at[:, dst, :], device))
-            cal_in[p].append(remote(cal_send.at[src, :], cal_buf.at[dst, :], device))
+            picked[p][NX - step] = remote(pick_send.at[:, src, :], row_buf.at[:, dst, :], device)
+            cal_in[p][NX - step] = remote(cal_send.at[src, :], cal_buf.at[dst, :], device)
 
     own_lanes = pl.ds(pl.multiple_of(c * DS, DS), DS)
     own_hid = pl.ds(pl.multiple_of(y * FC, 128), FC)
     left_y, right_y = lax.rem(y + NY - 1, NY), lax.rem(y + 1, NY)
     direct, to_self, forwarded, kept = {}, {}, {}, {}
 
-    def stage_spread(p):
-        arrive(picked[p])
-        rows = pl.ds(p * ROWS, ROWS)
-        direct[p] = [
+    def base(n):
+        return ORDER[n // 2] * ROWS + n % 2 * HALF
+
+    def slots(n):
+        return (2, 3) if n % 2 else (0, 1)
+
+    def stage_spread(n):
+        arrive(picked[ORDER[n // 2]][slot] for slot in slots(n) if slot)
+        rows = pl.ds(base(n), HALF)
+        direct[n] = [
             remote(row_buf.at[flip, rows, :], xs.at[rows, own_lanes], at_y(step, flip))
             for flip in range(2) for step in (1, -1)
         ]
-        to_self[p] = remote(row_buf.at[1, rows, :], xs.at[rows, own_lanes], sibling)
-        kept[p] = local(row_buf.at[0, rows, :], xs.at[rows, own_lanes])
-
-    def stage_forward(p):
-        arrive(direct[p])
-        half = ROWS // 2
-        a = (pl.ds(p * ROWS, half), pl.ds(pl.multiple_of(left_y * 2 * DS, DS), 2 * DS))
-        b = (pl.ds(p * ROWS + half, half), pl.ds(pl.multiple_of(right_y * 2 * DS, DS), 2 * DS))
-        forwarded[p] = [
+        to_self[n] = remote(row_buf.at[1, rows, :], xs.at[rows, own_lanes], sibling)
+        kept[n] = local(row_buf.at[0, rows, :], xs.at[rows, own_lanes])
+
+    def stage_forward(n):
+        arrive(direct[n])
+        half = HALF // 2
+        a = (pl.ds(base(n), half), pl.ds(pl.multiple_of(left_y * 2 * DS, DS), 2 * DS))
+        b = (pl.ds(base(n) + half, half), pl.ds(pl.multiple_of(right_y * 2 * DS, DS), 2 * DS))
+        forwarded[n] = [
             remote(xs.at[a], xs.at[a], at_y(1)),
             remote(xs.at[b], xs.at[b], at_y(-1)),
         ]
 
     hid_direct, hid_forwarded, hid_kept = {}, {}, {}
 
-    def stage_hidden(p):
-        if p == 0:
+    def stage_hidden(n):
+        if n == 0:
             for copy in weights_local[:2]:
                 copy.wait()
             arrive(weights_remote[:2])
-        arrive(forwarded[p])
-        to_self[p].wait_recv()
-        kept[p].wait()
-        arrive(cal_in[p])
-        rows = pl.ds(p * ROWS, ROWS)
+        arrive(forwarded[n])
+        to_self[n].wait_recv()
+        kept[n].wait()
+        arrive(cal_in[ORDER[n // 2]][slot] for slot in slots(n) if slot)
+        rows = pl.ds(base(n), HALF)
         both = lax.dot_general(
             xs[rows, :], w_in[...], (((1,), (1,)), ((), ())), preferred_element_type=F32
         )
         gate, up = both[:, 0:FC], both[:, FC : 2 * FC]
         h = (gate / (1.0 + jnp.exp(-gate)) * up).astype(BF16)
         hid_own[rows, :] = h
-        hid_direct[p] = [
+        hid_direct[n] = [
             remote(hid_own.at[rows, :], hid.at[rows, own_hid], at_y(step)) for step in (1, -1)
         ]
-        hid_kept[p] = local(hid_own.at[rows, :], hid.at[rows, own_hid])
+        hid_kept[n] = local(hid_own.at[rows, :], hid.at[rows, own_hid])
         cal = cal_buf[rows, :][:, 0:1].astype(F32)
         scaled[rows, :] = (cal * h.astype(F32)).astype(BF16)
 
-    def stage_hidden_forward(p):
-        arrive(hid_direct[p])
-        half = ROWS // 2
-        a = (pl.ds(p * ROWS, half), pl.ds(pl.multiple_of(left_y * FC, 128), FC))
-        b = (pl.ds(p * ROWS + half, half), pl.ds(pl.multiple_of(right_y * FC, 128), FC))
-        hid_forwarded[p] = [
+    def stage_hidden_forward(n):
+        arrive(hid_direct[n])
+        half = HALF // 2
+        a = (pl.ds(base(n), half), pl.ds(pl.multiple_of(left_y * FC, 128), FC))
+        b = (pl.ds(base(n) + half, half), pl.ds(pl.multiple_of(right_y * FC, 128), FC))
+        hid_forwarded[n] = [
             remote(hid.at[a], hid.at[a], at_y(1)),
             remote(hid.at[b], hid.at[b], at_y(-1)),
         ]
 
     returned, back_kept = {}, {}
 
-    def stage_down(p):
-        if p == 0:
+    def stage_down(n):
+        p = ORDER[n // 2]
+        if n == 0:
             weights_local[2].wait()
             arrive(weights_remote[2:])
-        arrive(hid_forwarded[p])
-        hid_kept[p].wait()
-        rows = pl.ds(p * ROWS, ROWS)
+        arrive(hid_forwarded[n])
+        hid_kept[n].wait()
+        rows = pl.ds(base(n), HALF)
         for flip in range(2):
             eo[flip, rows, :] = jnp.dot(
                 hid[rows, :], w_dn[flip], preferred_element_type=F32
             ).astype(BF16)
-        returned[p] = []
-        for step in range(NX):
+        returned.setdefault(p, [])
+        for step in slots(n):
             src = pl.ds(p * ROWS + step * PAIR, PAIR)
             dst = pl.ds(p * ROWS + (NX - step) % NX * PAIR, PAIR)
             for flip in range(2):
@@ -277,7 +287,7 @@
                 continue
             s = pl.ds((2 * p + b) * TOK, TOK)
             offset = p if b == 0 else -(p + 1)
-            parts.append(remote(part.at[s, :], part_in.at[s, :], at_z(offset)))
+            parts.append((s, remote(part.at[s, :], part_in.at[s, :], at_z(offset))))
 
     grams = []
 
@@ -290,40 +300,37 @@
         grams.append(remote(gram.at[theirs, :], gram_ref.at[k], sibling))
         grams.append(local(gram.at[mine, :], gram_ref.at[k]))
 
+    halves = 2 * CHUNKS
+    z_forward(1)
     stage_pick(0)
-    stage_pick(1)
-    stage_spread(0)
-    stage_pick(2)
-    stage_spread(1)
-    stage_pick(3)
-    stage_forward(0)
-    stage_spread(2)
-    stage_forward(1)
-    stage_hidden(0)
-    stage_spread(3)
-    stage_forward(2)
-    stage_hidden_forward(0)
-    stage_hidden(1)
-    stage_down(0)
-    stage_forward(3)
-    stage_hidden_forward(1)
-    stage_hidden(2)
-    stage_combine(0)
-    stage_down(1)
-    stage_hidden_forward(2)
-    stage_hidden(3)
-    stage_combine(1)
-    stage_down(2)
-    stage_hidden_forward(3)
-    stage_combine(2)
-    stage_down(3)
-    stage_gram()
-    stage_combine(3)
+    z_forward(2)
+    for n in range(halves + 5):
+        if n < halves:
+            stage_spread(n)
+        if n == 1:
+            z_forward(3)
+            stage_pick(ORDER[1])
+        if 1 <= n <= halves:
+            stage_forward(n - 1)
+        if n == 1:
+            z_forward(4)
+        if n in (2, 4):
+            stage_pick(ORDER[n // 2 + 1])
+        if 2 <= n < halves + 2:
+            stage_hidden(n - 2)
+        if 3 <= n < halves + 3:
+            stage_hidden_forward(n - 3)
+        if 4 <= n < halves + 4:
+            stage_down(n - 4)
+        if n == halves + 4:
+            stage_gram()
+        if n >= 6 and n % 2 == 0:
+            stage_combine(ORDER[n // 2 - 3])
 
     total = part[pl.ds(0, TOK), :].astype(F32)
-    for n, copy in enumerate(parts):
+    for s, copy in parts:
         copy.wait_recv()
-        total = total + part_in[pl.ds((n + 1) * TOK, TOK), :].astype(F32)
+        total = total + part_in[s, :].astype(F32)
     out_ref[...] = total.astype(BF16)
     grams[0].wait_recv()
     grams[1].wait()
@@ -369,7 +376,7 @@
             pltpu.VMEM((FC, FF), F32),
             pltpu.SemaphoreType.DMA((NSEM,)),
             pltpu.SemaphoreType.DMA((NSEM,)),
-            pltpu.SemaphoreType.DMA((24,)),
+            pltpu.SemaphoreType.DMA((40,)),
         ],
         compiler_params=pltpu.CompilerParams(
             collective_id=0, has_side_effects=True, vmem_limit_bytes=60 * 1024 * 1024

time: 140 us -> 128 us (0.914)
  Pallas kernels: 131 us -> 119 us
    pallas_call x1, Pallas kernels: 131 us -> 119 us  [on_device(): pl.pallas_call(kernel, out_shape=(jax.ShapeDtypeStruct((TOK, DS), BF16),...]
where the time goes in v2:
time: 128 us; the launch traced here: 127 us
  Pallas kernels  119 us (93%)
  local copies, waits for them, and re-layouts  4.87 us (4%)
  other arithmetic  2.81 us (2%)
    pallas_call x1, Pallas kernels, on_device(): pl.pallas_call(kernel, out_shape=(jax.ShapeDtypeStruct((TOK, DS), BF16),...  119 us
    unnamed x2, local copies, waits for them, and re-layouts  4.79 us

profile of v2, /device:TPU:1, one launch (start us, length us, event | category | flops | bytes accessed | tf_op | source)
XLA Modules:
  0.0 127.4 jit_solution(4971645233488317830)
XLA Ops:
  0.6 0.8 select_reduce_fusion
  1.4 0.1 pad.3.clone
  1.5 0.7 convert_bitcast_fusion
  2.2 1.4 %maximum_maximum_fusion.meta_hbm = f32[24,128]{1,0:T(8,128)} fusion(f32[1,128]{1,0:T(1,128)S(1)} %bitcast.5, f32[8,128]{1,0:T(8,128)} %bitcast.4, f32[8,128]{1,0:T(8,128)S(1)} %convert_bitcast_fusion, f32[24]{0:T(128)S(1)} %pad.3.clone), kind=kLoop, calls=%fused_computation.2 | loop fusion | flops 9216 | bytes 21088 | tf_op jit(solution)/shard_map/concatenate | solution.py:344
  3.5 119.0 %routed_experts.1 = (bf16[128,512]{1,0:T(8,128)(2,1)}, f32[2,192,1536]{2,1,0:T(8,128)}) custom-call(bf16[128,512]{1,0:T(8,128)(2,1)} %tok_hbm.1, f32[24,128]{1,0:T(8,128)} %maximum_maximum_fusion.meta_hbm, bf16[2,192,4096]{2,1,0:T(8,128)(2,1)} %wg_hbm.1, bf16[2,192,4096]{2,1,0:T(8,128)(2,1)} %wu_hbm.1, bf16[2,1536,512]{2,1,0:T(8,128)(2,1)} %wd_hbm.1), custom_call_target="tpu_custom_call" | custom-call | tf_op jit(solution)/shard_map/routed_experts/pallas_call | solution.py:349
  122.6 1.6 %copy.12 = bf16[128,512]{1,0:T(8,128)(2,1)} copy(bf16[128,512]{1,0:T(8,128)(2,1)} %get-tuple-element.4) | data formatting | bytes 262144
  124.1 3.2 %copy.13 = f32[2,192,1536]{2,1,0:T(8,128)} copy(f32[2,192,1536]{2,1,0:T(8,128)} %get-tuple-element.5) | data formatting | bytes 4718592
  (1 shorter events, 0.0 us)

commit v3 on v2

--- a/solution.py
+++ b/solution.py
@@ -13,7 +13,7 @@
 ROWS = NX * PAIR
 CHUNKS = NZ // 2
 HALF = ROWS // 2
-ORDER = (0, 2, 3, 1)
+ORDER = (0, 3, 2, 1)
 D = 4096
 DS = 512
 FF = 1536
@@ -185,11 +185,14 @@
     left_y, right_y = lax.rem(y + NY - 1, NY), lax.rem(y + 1, NY)
     direct, to_self, forwarded, kept = {}, {}, {}, {}
 
+    def second(n):
+        return 1 - n % 2 if n // 2 == CHUNKS - 1 else n % 2
+
     def base(n):
-        return ORDER[n // 2] * ROWS + n % 2 * HALF
+        return ORDER[n // 2] * ROWS + second(n) * HALF
 
     def slots(n):
-        return (2, 3) if n % 2 else (0, 1)
+        return (2, 3) if second(n) else (0, 1)
 
     def stage_spread(n):
         arrive(picked[ORDER[n // 2]][slot] for slot in slots(n) if slot)
@@ -279,15 +282,22 @@
         back_kept[p].wait()
         rows = back[:, pl.ds(p * ROWS, ROWS), :].reshape(2 * ROWS, DS)
         dims = (((0,), (0,)), ((), ()))
-        total = lax.dot_general(coef_hi[p], rows, dims, preferred_element_type=F32)
-        total = total + lax.dot_general(coef_lo[p], rows, dims, preferred_element_type=F32)
-        part[pl.ds(2 * p * TOK, 2 * TOK), :] = total.astype(BF16)
-        for b in range(2):
-            if p == 0 and b == 0:
-                continue
-            s = pl.ds((2 * p + b) * TOK, TOK)
-            offset = p if b == 0 else -(p + 1)
-            parts.append((s, remote(part.at[s, :], part_in.at[s, :], at_z(offset))))
+        for blocks in ((1,), (0,)) if p == ORDER[-1] else ((0, 1),):
+            lanes = slice(blocks[0] * TOK, (blocks[-1] + 1) * TOK)
+            total = lax.dot_general(
+                coef_hi[p, :, lanes], rows, dims, preferred_element_type=F32
+            )
+            total = total + lax.dot_general(
+                coef_lo[p, :, lanes], rows, dims, preferred_element_type=F32
+            )
+            into = pl.ds((2 * p + blocks[0]) * TOK, len(blocks) * TOK)
+            part[into, :] = total.astype(BF16)
+            for b in blocks:
+                if p == 0 and b == 0:
+                    continue
+                s = pl.ds((2 * p + b) * TOK, TOK)
+                offset = p if b == 0 else -(p + 1)
+                parts.append((s, remote(part.at[s, :], part_in.at[s, :], at_z(offset))))
 
     grams = []
 
@@ -305,17 +315,20 @@
     stage_pick(0)
     z_forward(2)
     for n in range(halves + 5):
-        if n < halves:
+        if n < halves and n != 2:
             stage_spread(n)
         if n == 1:
             z_forward(3)
-            stage_pick(ORDER[1])
         if 1 <= n <= halves:
             stage_forward(n - 1)
         if n == 1:
             z_forward(4)
-        if n in (2, 4):
-            stage_pick(ORDER[n // 2 + 1])
+            stage_pick(ORDER[1])
+        if n == 2:
+            stage_pick(ORDER[2])
+            stage_spread(n)
+        if n == 4:
+            stage_pick(ORDER[3])
         if 2 <= n < halves + 2:
             stage_hidden(n - 2)
         if 3 <= n < halves + 3:

time: 128 us -> 128 us (level)
  no operation moved by 1% of the time
where the time goes in v3:
time: 128 us; the launch traced here: 127 us
  Pallas kernels  119 us (93%)
  local copies, waits for them, and re-layouts  4.87 us (4%)
  other arithmetic  2.81 us (2%)
    pallas_call x1, Pallas kernels, on_device(): pl.pallas_call(kernel, out_shape=(jax.ShapeDtypeStruct((TOK, DS), BF16),...  119 us
    unnamed x2, local copies, waits for them, and re-layouts  4.79 us

profile of v3, /device:TPU:1, one launch (start us, length us, event | category | flops | bytes accessed | tf_op | source)
XLA Modules:
  0.0 127.4 jit_solution(4686665289255872859)
XLA Ops:
  0.6 0.8 select_reduce_fusion
  1.4 0.1 pad.3.clone
  1.5 0.7 convert_bitcast_fusion
  2.2 1.4 %maximum_maximum_fusion.meta_hbm = f32[24,128]{1,0:T(8,128)} fusion(f32[1,128]{1,0:T(1,128)S(1)} %bitcast.5, f32[8,128]{1,0:T(8,128)} %bitcast.4, f32[8,128]{1,0:T(8,128)S(1)} %convert_bitcast_fusion, f32[24]{0:T(128)S(1)} %pad.3.clone), kind=kLoop, calls=%fused_computation.2 | loop fusion | flops 9216 | bytes 21088 | tf_op jit(solution)/shard_map/concatenate | solution.py:357
  3.5 119.1 %routed_experts.1 = (bf16[128,512]{1,0:T(8,128)(2,1)}, f32[2,192,1536]{2,1,0:T(8,128)}) custom-call(bf16[128,512]{1,0:T(8,128)(2,1)} %tok_hbm.1, f32[24,128]{1,0:T(8,128)} %maximum_maximum_fusion.meta_hbm, bf16[2,192,4096]{2,1,0:T(8,128)(2,1)} %wg_hbm.1, bf16[2,192,4096]{2,1,0:T(8,128)(2,1)} %wu_hbm.1, bf16[2,1536,512]{2,1,0:T(8,128)(2,1)} %wd_hbm.1), custom_call_target="tpu_custom_call" | custom-call | tf_op jit(solution)/shard_map/routed_experts/pallas_call | solution.py:362
  122.6 1.6 %copy.12 = bf16[128,512]{1,0:T(8,128)(2,1)} copy(bf16[128,512]{1,0:T(8,128)(2,1)} %get-tuple-element.4) | data formatting | bytes 262144
  124.2 3.2 %copy.13 = f32[2,192,1536]{2,1,0:T(8,128)} copy(f32[2,192,1536]{2,1,0:T(8,128)} %get-tuple-element.5) | data formatting | bytes 4718592
  (1 shorter events, 0.0 us)

commit v4 on v3

--- a/solution.py
+++ b/solution.py
@@ -26,9 +26,9 @@
 
 
 def kernel(
-    tok_hbm, meta_hbm, wg_hbm, wu_hbm, wd_hbm,
+    tok_hbm, routes_hbm, gains_hbm, cal_hbm, wg_hbm, wu_hbm, wd_hbm,
     out_ref, gram_ref,
-    tok, meta, pick_send, row_buf, cal_send, cal_buf, xs, w_in, w_dn,
+    tok, routes, gains, cals, meta, pick_send, row_buf, cal_send, cal_buf, xs, w_in, w_dn,
     hid_own, scaled, hid, eo, back, coef_hi, coef_lo, part, part_in, gram,
     send_sem, recv_sem, local_sem,
 ):
@@ -77,7 +77,7 @@
             copy.wait_recv()
 
     own_tok = local(tok_hbm, tok.at[pl.ds(0, TOK), :])
-    own_meta = local(meta_hbm, meta.at[0])
+    own_meta = [local(routes_hbm, routes), local(gains_hbm, gains), local(cal_hbm, cals)]
     own_rows = pl.ds(pl.multiple_of(k * FS, 64), FS)
     own_rows_up = pl.ds(pl.multiple_of(FC + k * FS, 64), FS)
     weights_local = [
@@ -93,6 +93,11 @@
     partners += [sibling]
     for device in partners:
         pl.semaphore_signal(barrier, inc=1, device_id=device, device_id_type=MESH)
+    for copy in own_meta:
+        copy.wait()
+    meta[0] = jnp.concatenate(
+        [routes[...].astype(F32), gains[...], jnp.broadcast_to(cals[...], (8, TOK))], axis=0
+    )
     pl.semaphore_wait(barrier, len(partners))
 
     def slot_of(offset):
@@ -107,7 +112,6 @@
         ]
 
     own_tok.wait()
-    own_meta.wait()
     right = {1: z_send(0, -1, 1)}
     left = {1: z_send(0, 1, -1)}
 
@@ -354,9 +358,6 @@
 def on_device(tokens, routes, route_weight, language, lang_weight, w_gate, w_up, w_down):
     langs = jnp.arange(lang_weight.shape[0], dtype=jnp.int32)
     cal = jnp.sum(jnp.where(language[None, :] == langs[:, None], lang_weight[:, None], 0.0), axis=0)
-    meta = jnp.concatenate(
-        [routes.T.astype(F32), route_weight.T, cal[None, :], jnp.zeros((7, TOK), F32)], axis=0
-    )
     rows = CHUNKS * ROWS
     anywhere = pl.BlockSpec(memory_space=pl.ANY)
     return pl.pallas_call(
@@ -365,10 +366,13 @@
             jax.ShapeDtypeStruct((TOK, DS), BF16),
             jax.ShapeDtypeStruct((2, FS, FF), F32),
         ),
-        in_specs=[anywhere] * 5,
+        in_specs=[anywhere] * 7,
         out_specs=(pl.BlockSpec(memory_space=pltpu.VMEM), anywhere),
         scratch_shapes=[
             pltpu.VMEM((NZ * TOK, DS), BF16),
+            pltpu.VMEM((8, TOK), jnp.int32),
+            pltpu.VMEM((8, TOK), F32),
+            pltpu.VMEM((1, TOK), F32),
             pltpu.VMEM((NZ, 24, TOK), F32),
             pltpu.VMEM((2, rows, DS), BF16),
             pltpu.VMEM((2, rows, DS), BF16),
@@ -395,7 +399,7 @@
             collective_id=0, has_side_effects=True, vmem_limit_bytes=60 * 1024 * 1024
         ),
         name="routed_experts",
-    )(tokens, meta, w_gate, w_up, w_down)
+    )(tokens, routes.T, route_weight.T, cal[None, :], w_gate, w_up, w_down)
 
 
 def solution(mesh):

time: 128 us -> 126 us (0.984)
  other arithmetic: 2.81 us -> 1.28 us
    concatenate x1 -> x0, other arithmetic: 1.36 us -> none  [on_device(): jnp.concatenate([routes.T.astype(F32), route_weight.T, cal[None, :], jnp....]
where the time goes in v4:
time: 126 us
  Pallas kernels  119 us (94%)
  local copies, waits for them, and re-layouts  4.79 us (4%)
  other arithmetic  1.28 us (1%)
    pallas_call x1, Pallas kernels, on_device(): pl.pallas_call(kernel, out_shape=(jax.ShapeDtypeStruct((TOK, DS), BF16),...  119 us
    unnamed x2, local copies, waits for them, and re-layouts  4.79 us

profile of v4, /device:TPU:1, one launch (start us, length us, event | category | flops | bytes accessed | tf_op | source)
XLA Modules:
  0.0 125.8 jit_solution(4502202267653994532)
XLA Ops:
  0.6 1.3 %select_reduce_fusion = f32[128]{0:T(128)} fusion(f32[119]{0:T(128)} %param.12, s32[128]{0:T(128)} %param.11), kind=kLoop, calls=%fused_computation | loop fusion | flops 45568 | bytes 1500 | tf_op jit(solution)/shard_map/reduce_sum | solution.py:360
  1.9 119.0 %routed_experts.1 = (bf16[128,512]{1,0:T(8,128)(2,1)}, f32[2,192,1536]{2,1,0:T(8,128)}) custom-call(bf16[128,512]{1,0:T(8,128)(2,1)} %tok_hbm.1, s32[8,128]{1,0:T(8,128)} %bitcast.3, f32[8,128]{1,0:T(8,128)} %bitcast.4, f32[1,128]{1,0:T(1,128)} %bitcast.5, bf16[2,192,4096]{2,1,0:T(8,128)(2,1)} %wg_hbm.1, bf16[2,192,4096]{2,1,0:T(8,128)(2,1)} %wu_hbm.1, ...), custom_call_target="tpu_custom_call" | custom-call | tf_op jit(solution)/shard_map/routed_experts/pallas_call | solution.py:363
  121.0 1.6 %copy.12 = bf16[128,512]{1,0:T(8,128)(2,1)} copy(bf16[128,512]{1,0:T(8,128)(2,1)} %get-tuple-element.4) | data formatting | bytes 262144
  122.5 3.2 %copy.13 = f32[2,192,1536]{2,1,0:T(8,128)} copy(f32[2,192,1536]{2,1,0:T(8,128)} %get-tuple-element.5) | data formatting | bytes 4718592
